TPU v7x, 32 devices: a whole 2x2x4 slice. The times are simulated.
32 devices in a mesh: gx: 8 (over y, x, core), gy: 4 (over z).
Axes of the slice: x: 2, y: 2, z: 4, core: 2. Of those that a mesh axis runs over, the one named last changes fastest.
Arguments:
- pressure: float32 [128, 256, 512], P('gx', 'gy'), may hold values from -3 to 3
- permeability: float32 [128, 256, 512], P('gx', 'gy'), may hold values from 0.1 to 1
- kernel: float32 [2, 1536, 1536], P(None, 'gx', 'gy'), may hold values from -1.2247449 to 1.2247449
- slip_rate: float32 [1536], P(('gx', 'gy')), may hold values from 0.1 to 1
- aging_state: float32 [1536], P(('gx', 'gy')), may hold values from 0.5 to 5
- normal_stress: float32 [1536], P(('gx', 'gy')), may hold values from 50 to 80
- shear_stress: float32 [1536], P(('gx', 'gy')), may hold values from 33 to 45
- direct_effect: float32 [1536], P(('gx', 'gy')), may hold values from 0.01 to 0.02
- evolution_effect: float32 [1536], P(('gx', 'gy')), may hold values from 0.01 to 0.03
- slip_distance: float32 [1536], P(('gx', 'gy')), may hold values from 0.2 to 1
- tri_owner: int32 [1536, 1], P(('gx', 'gy')), may hold values from 0 to 7; in each aligned block of 48 rows (0 to 47, 48 to 95, ...) at most 12 rows name the same one
- tri_cell: int32 [1536], P(('gx', 'gy')), may hold values from 0 to 524287
Outputs:
- pressure_next: float32 [128, 256, 512], P('gx', 'gy')
- state_next: float32 [1536], P(('gx', 'gy'))
- log_rate: float32 [1536], P(('gx', 'gy'))
Inputs may be any that keep to these rules, and one draw needn't show every extreme that they name: `tri_owner`: at most 12 of the 48 triangles of one device name one owner, and in every draw some owner is named by exactly 12 triangles of some device.
All inputs are finite; a program needn't handle non-finite values.
Results may differ from a plain program's by a relative error of at most 0.000092.
Values sent between devices are 32-bit elements; how exact they have to be, the bound alone decides.
A program may use at most 64 MiB of HBM per device.

v0:
```python
import jax
import jax.numpy as jnp
from jax import lax
from jax.sharding import PartitionSpec as P

SWEEPS = 3


conductance = 0.15
step_time = 1.0
heal_time = 0.5
friction_ref = 0.6
neighbours = ((1, 0, 0), (-1, 0, 0), (0, 1, 0), (0, -1, 0), (0, 0, 1), (0, 0, -1))


def padded(value, sides, width):
    for axis, dim in sides:
        count, length = (lax.axis_size(axis), value.shape[dim])
        up = [(i, (i + 1) % count) for i in range(count - 1)]
        down = [(j, i) for i, j in up]
        last = lax.slice_in_dim(value, length - width, length, axis=dim)
        leading = lax.slice_in_dim(value, 0, width, axis=dim)
        before = lax.ppermute(last, axis, up)
        after = lax.ppermute(leading, axis, down)
        value = jnp.concatenate([before, value, after], axis=dim)
    return value


def shifted(values, step_x, step_y, step_z):
    return values[
        1 + step_x : values.shape[0] - 1 + step_x,
        1 + step_y : values.shape[1] - 1 + step_y,
        1 + step_z : values.shape[2] - 1 + step_z,
    ]


def explicit_step(padded_p, padded_k):
    full_p = jnp.pad(padded_p, ((0, 0), (0, 0), (1, 1)))
    full_k = jnp.pad(padded_k, ((0, 0), (0, 0), (1, 1)))
    centre_p = shifted(full_p, 0, 0, 0)
    centre_k = shifted(full_k, 0, 0, 0)
    flux = jnp.zeros_like(centre_p)
    for offset in neighbours:
        other_p = shifted(full_p, offset[0], offset[1], offset[2])
        other_k = shifted(full_k, offset[0], offset[1], offset[2])
        flux = flux + jnp.sqrt(centre_k * other_k) * (other_p - centre_p)
    return centre_p + conductance * flux


def diffuse(pressure, permeability):
    padded_p, padded_k = (
        padded(pressure, (("gx", 0), ("gy", 1)), SWEEPS),
        padded(permeability, (("gx", 0), ("gy", 1)), SWEEPS),
    )
    for repeat in range(SWEEPS):
        padded_p = explicit_step(padded_p, padded_k)
        padded_k = padded_k[1:-1, 1:-1]
    return padded_p


def tractions(kernel, slip_rate):
    gathered = lax.all_gather(slip_rate, ("gx", "gy"), axis=0, tiled=True)
    column_count = kernel.shape[2]
    offset = lax.axis_index("gy") * column_count
    segment = lax.dynamic_slice_in_dim(gathered, offset, column_count, 0)
    partial_value = jnp.dot(
        kernel.reshape(-1, column_count), segment, precision=lax.Precision.HIGHEST
    ).reshape(2, kernel.shape[1])
    return lax.psum_scatter(partial_value, "gy", scatter_dimension=1, tiled=True)


def fault_pressure_of(pressure_field, tri_owner, tri_cell):
    owners = tri_owner[:, 0]
    tri_count = owners.shape[0]
    groups = lax.axis_size("gx")
    capacity = max(2, 2 * tri_count // groups)
    same_owner = owners[:, None] == owners[None, :]
    indices = jnp.arange(tri_count, dtype=jnp.int32)
    earlier = indices[None, :] < indices[:, None]
    slot_rank = jnp.sum(jnp.logical_and(same_owner, earlier), axis=1)
    slot_index = owners * capacity + slot_rank
    matches = slot_index[:, None] == jnp.arange(groups * capacity, dtype=jnp.int32)[None, :]
    requests = jnp.sum(jnp.where(matches, tri_cell[:, None], 0), axis=0).reshape(groups, capacity)
    flat_field = pressure_field.reshape(-1)
    values = jnp.take(
        flat_field, lax.all_to_all(requests, "gx", split_axis=0, concat_axis=0, tiled=True), axis=0
    )
    answers = lax.all_to_all(values, "gx", split_axis=0, concat_axis=0, tiled=True)
    return jnp.sum(jnp.where(matches, answers.reshape(-1)[None, :], 0.0), axis=1)


def local(
    pressure,
    permeability,
    kernel,
    slip_rate,
    aging_state,
    normal_stress,
    shear_stress,
    direct_effect,
    evolution_effect,
    slip_distance,
    tri_owner,
    tri_cell,
):
    pressure_field = diffuse(pressure, permeability)
    rates = tractions(kernel, slip_rate)
    fault_pressure = fault_pressure_of(pressure_field, tri_owner, tri_cell)
    shear = shear_stress + step_time * rates[0]
    effective = normal_stress + step_time * rates[1] - fault_pressure
    ratio = slip_distance / slip_rate
    state_next = ratio + (aging_state - ratio) * jnp.exp(-heal_time / ratio)
    log_rate = (
        shear / effective - friction_ref - evolution_effect * jnp.log(state_next / slip_distance)
    ) / direct_effect
    return (pressure_field, state_next, log_rate)


def solution(mesh):
    in_specs = (
        P("gx", "gy", None),
        P("gx", "gy", None),
        P(None, "gx", "gy"),
        P(("gx", "gy")),
        P(("gx", "gy")),
        P(("gx", "gy")),
        P(("gx", "gy")),
        P(("gx", "gy")),
        P(("gx", "gy")),
        P(("gx", "gy")),
        P(("gx", "gy"), None),
        P(("gx", "gy")),
    )
    out_specs = (P("gx", "gy", None), P(("gx", "gy")), P(("gx", "gy")))
    return jax.shard_map(local, mesh=mesh, in_specs=in_specs, out_specs=out_specs, check_vma=False)
```

profile of v0, /device:TPU:0, one launch (start us, length us, event | category | flops | bytes accessed | tf_op | source)
XLA Modules:
  0.0 164.4 jit_solution(4125248963078330247)
XLA Ops:
  7.2 2.2 %fusion.84 = (f32[3,64,512]{2,1,0:T(8,128)}, f32[3,64,512]{2,1,0:T(8,128)}) fusion(f32[16,64,512]{2,1,0:T(8,128)} %param.13), kind=kLoop, calls=%fused_computation.147 | loop fusion | bytes 1572864 | tf_op jit(solution)/shard_map/slice | solution.py:22
  9.5 2.4 %collective-permute-start.4 = (f32[3,64,512]{2,1,0:T(8,128)}, f32[3,64,512]{2,1,0:T(8,128)S(1)}, u32[]{:S(2)}, u32[]{:S(2)}) collective-permute-start(f32[3,64,512]{2,1,0:T(8,128)} %get-tuple-element.16), channel_id=1, source_target_pairs={{0,4},{4,8},{8,12},{12,16},{16,20},{20,24},{24,28},{1,5},{5,9},{9,... | collective-permute-start | bytes 1179656 | tf_op jit(solution)/shard_map/ppermute | solution.py:23
  11.9 1.3 collective-permute-start.5
  13.2 2.1 %fusion.83 = (f32[3,64,512]{2,1,0:T(8,128)}, f32[3,64,512]{2,1,0:T(8,128)}) fusion(f32[16,64,512]{2,1,0:T(8,128)} %param.12), kind=kLoop, calls=%fused_computation.146 | loop fusion | bytes 1572864 | tf_op jit(solution)/shard_map/slice | solution.py:22
  15.3 5.9 %collective-permute-start = (f32[3,64,512]{2,1,0:T(8,128)}, f32[3,64,512]{2,1,0:T(8,128)}, u32[]{:S(2)}, u32[]{:S(2)}) collective-permute-start(f32[3,64,512]{2,1,0:T(8,128)} %get-tuple-element.14), channel_id=1, source_target_pairs={{0,4},{4,8},{8,12},{12,16},{16,20},{20,24},{24,28},{1,5},{5,9},{9,... | collective-permute-start | bytes 1179656 | tf_op jit(solution)/shard_map/ppermute | solution.py:23
  21.2 1.3 collective-permute-start.1
  22.5 0.2 convert_reduce_fusion
  22.7 0.5 copy-done.23
  23.2 0.1 select_reduce_fusion.1
  23.3 0.7 all_to_all.12
  23.9 6.3 %all-to-all-start = ((s32[8,1,12]{2,1,0:T(1,128)}), s32[8,1,12]{2,1,0:T(1,128)S(1)}, u32[]{:S(2)}, u32[]{:S(2)}) async-start(s32[8,1,12]{2,1,0:T(1,128)} %bitcast.6), calls=%async_computation | async-start | bytes 8192 | tf_op jit(solution)/shard_map/all_to_all | solution.py:86
  30.3 0.3 dynamic-update-slice
  30.6 40.8 %all-reduce.6 = f32[1536]{0:T(1024)S(1)} all-reduce(f32[1536]{0:T(1024)S(1)} %dynamic-update-slice), channel_id=1, replica_groups=mesh['gx'=8,'gy'=4] {'gx','gy'}, use_global_device_ids=true, to_apply=%add.6 | all-reduce | flops 1536 | bytes 12288
  71.5 0.1 dynamic_slice.3
  71.5 0.7 fusion.86
  72.3 0.8 copy.26
  73.1 0.1 reshape.62
  73.3 0.2 constant_dynamic-update-slice_fusion.4
  73.5 0.4 copy-done.9
  74.0 3.7 %collective-permute-start.6 = (f32[22,3,512]{2,1,0:T(4,128)S(1)}, f32[22,3,512]{2,1,0:T(4,128)S(1)}, u32[]{:S(2)}, u32[]{:S(2)}) collective-permute-start(f32[22,3,512]{2,1,0:T(4,128)S(1)} %get-tuple-element.11), channel_id=1, source_target_pairs={{0,1},{1,2},{2,3},{4,5},{5,6},{6,7},{8,9},{9,10},{10,11},{12,13},{... | collective-permute-start | bytes 405512 | tf_op jit(solution)/shard_map/ppermute | solution.py:23
  77.7 1.3 collective-permute-start.7
  79.0 1.0 constant_dynamic-update-slice_fusion.2
  80.1 0.2 constant_dynamic-update-slice_fusion.1
  80.3 1.0 constant_dynamic-update-slice_fusion
  81.4 4.6 %collective-permute-start.2 = (f32[22,3,512]{2,1,0:T(4,128)S(1)}, f32[22,3,512]{2,1,0:T(4,128)S(1)}, u32[]{:S(2)}, u32[]{:S(2)}) collective-permute-start(f32[22,3,512]{2,1,0:T(4,128)S(1)} %get-tuple-element.9), channel_id=1, source_target_pairs={{0,1},{1,2},{2,3},{4,5},{5,6},{6,7},{8,9},{9,10},{10,11},{12,13},{... | collective-permute-start | bytes 405512 | tf_op jit(solution)/shard_map/ppermute | solution.py:23
  85.9 1.5 collective-permute-start.3
  87.5 0.6 pad_maximum_fusion.1
  88.1 0.1 copy-done.5
  88.2 0.2 copy-done.7
  88.4 0.8 collective-permute-done.2
  89.2 4.2 %collective-permute-done.3 = f32[22,3,512]{2,1,0:T(4,128)S(1)} collective-permute-done((f32[22,3,512]{2,1,0:T(4,128)S(1)}, f32[22,3,512]{2,1,0:T(4,128)S(1)}, u32[]{:S(2)}, u32[]{:S(2)}) %collective-permute-start.3) | collective-permute-done | bytes 135200 | tf_op jit(solution)/shard_map/ppermute | solution.py:24
  93.4 2.1 %pad_maximum_fusion = f32[22,70,512]{2,1,0:T(8,128)} fusion(f32[22,3,512]{2,1,0:T(4,128)S(1)} %collective-permute-done.3, f32[22,64,512]{2,1,0:T(8,128)S(1)} %constant_dynamic-update-slice_fusion, f32[22,3,512]{2,1,0:T(4,128)S(1)} %collective-permute-done.2), kind=kLoop, calls=%fused_computation.13 | loop fusion | flops 1576960 | bytes 6307840 | tf_op jit(solution)/shard_map/concatenate | solution.py:25
  95.5 20.1 %fusion.6 = (f32[20,68,512]{2,1,0:T(8,128)}, f32[20,68,512]{2,1,0:T(8,128)}) fusion(f32[22,70,512]{2,1,0:T(8,128)S(1)} %pad_maximum_fusion.1, f32[22,70,512]{2,1,0:T(8,128)} %pad_maximum_fusion), kind=kLoop, calls=%fused_computation.25 | loop fusion | flops 17408000 | bytes 41549824 | tf_op jit(solution)/shard_map/add | solution.py:47
  115.7 16.8 %fusion.31 = (f32[18,66,512]{2,1,0:T(8,128)S(1)}, f32[18,66,512]{2,1,0:T(8,128)S(1)}) fusion(f32[22,3,512]{2,1,0:T(4,128)} %copy-done.5, f32[22,64,512]{2,1,0:T(8,128)S(1)} %constant_dynamic-update-slice_fusion.3, f32[22,3,512]{2,1,0:T(4,128)} %copy-done.7, f32[20,68,512]{2,1,0:T(8,128)} %get-tuple-element.8, f32[20,68,512]{2,1,0:T(8,128)} %get-tuple-element.7, ...), kind=kLoop, calls=%fused_computation.58 | loop fusion | flops 16422912 | bytes 34578432 | tf_op jit(solution)/shard_map/add | solution.py:47
  132.6 10.9 %fusion.56 = f32[16,64,512]{2,1,0:T(8,128)S(1)} fusion(f32[16,64,512]{2,1,0:T(8,128)S(1)} %copy-done.2, f32[18,66,512]{2,1,0:T(8,128)S(1)} %get-tuple-element.6, f32[18,66,512]{2,1,0:T(8,128)S(1)} %get-tuple-element.5, f32[22,64,512]{2,1,0:T(8,128)S(1)} %constant_dynamic-update-slice_fusion.3, f32[22,3,512]{2,1,0:T(4,128)S(1)} %copy-done.6, ...), kind=kLoop, calls=%fused_computation.89 | loop fusion | flops 15204352 | bytes 24018944 | tf_op jit(solution)/shard_map/add | solution.py:47
  143.5 1.3 copy-done.3
  144.8 0.5 copy.30
  145.5 1.1 gather_fusion
  146.6 0.1 gather.7
  146.7 0.6 and_select_fusion
  147.3 3.6 %all-to-all-start.1 = ((f32[8,1,12]{2,1,0:T(1,128)}), f32[8,1,12]{2,1,0:T(1,128)S(1)}, u32[]{:S(2)}, u32[]{:S(2)}) async-start(f32[8,1,12]{2,1,0:T(1,128)} %bitcast.11), calls=%async_computation.1 | async-start | bytes 8192 | tf_op jit(solution)/shard_map/all_to_all | solution.py:88
  150.9 0.9 fusion.85
  151.9 3.6 %all-to-all-done.1 = f32[8,1,12]{2,1,0:T(1,128)S(1)} async-done(((f32[8,1,12]{2,1,0:T(1,128)}), f32[8,1,12]{2,1,0:T(1,128)S(1)}, u32[]{:S(2)}, u32[]{:S(2)}) %all-to-all-start.1) | async-done | bytes 416 | tf_op jit(solution)/shard_map/all_to_all | solution.py:88
  155.5 0.5 broadcast.56
  156.1 0.7 reduce.3
  156.7 0.1 broadcast_in_dim.40
  156.8 0.2 select_reduce_fusion
  157.1 0.5 subtract_divide_fusion
  (67 shorter events, 0.6 us)
Async XLA Ops:
  7.2 64.4 %copy-start = (f32[2,192,384]{2,1,0:T(8,128)S(1)}, f32[2,192,384]{2,1,0:T(8,128)}, u32[]{:S(2)}) copy-start(f32[2,192,384]{2,1,0:T(8,128)} %param.14) | copy-start | bytes 1769476
  7.2 66.1 %copy-start.1 = (f32[16,64,512]{2,1,0:T(8,128)S(1)}, f32[16,64,512]{2,1,0:T(8,128)}, u32[]{:S(2)}) copy-start(f32[16,64,512]{2,1,0:T(8,128)} %param.13) | copy-start | bytes 6291460
  7.2 15.3 %copy-start.21 = (s32[48,1]{0,1:T(1,128)S(1)}, s32[48,1]{0,1:T(1,128)}, u32[]{:S(2)}) copy-start(s32[48,1]{0,1:T(1,128)} %param.22) | copy-start | bytes 580
  7.2 16.0 %copy-start.22 = (s32[48]{0:T(128)S(1)}, s32[48]{0:T(128)}, u32[]{:S(2)}) copy-start(s32[48]{0:T(128)} %param.23) | copy-start | bytes 580
  7.2 23.1 %copy-start.17 = (f32[48]{0:T(128)S(1)}, f32[48]{0:T(128)}, u32[]{:S(2)}) copy-start(f32[48]{0:T(128)} %param.15) | copy-start | bytes 580
  9.5 63.7 %collective-permute-start.4 = (f32[3,64,512]{2,1,0:T(8,128)}, f32[3,64,512]{2,1,0:T(8,128)S(1)}, u32[]{:S(2)}, u32[]{:S(2)}) collective-permute-start(f32[3,64,512]{2,1,0:T(8,128)} %get-tuple-element.16), channel_id=1, source_target_pairs={{0,4},{4,8},{8,12},{12,16},{16,20},{20,24},{24,28},{1,5},{5,9},{9,... | collective-permute-start | bytes 1179656 | tf_op jit(solution)/shard_map/ppermute | solution.py:23
  11.9 61.6 %collective-permute-start.5 = (f32[3,64,512]{2,1,0:T(8,128)}, f32[3,64,512]{2,1,0:T(8,128)S(1)}, u32[]{:S(2)}, u32[]{:S(2)}) collective-permute-start(f32[3,64,512]{2,1,0:T(8,128)} %get-tuple-element.15), channel_id=1, source_target_pairs={{4,0},{8,4},{12,8},{16,12},{20,16},{24,20},{28,24},{5,1},{9,5},{13... | collective-permute-start | bytes 1179656 | tf_op jit(solution)/shard_map/ppermute | solution.py:24
  15.3 63.7 %collective-permute-start = (f32[3,64,512]{2,1,0:T(8,128)}, f32[3,64,512]{2,1,0:T(8,128)}, u32[]{:S(2)}, u32[]{:S(2)}) collective-permute-start(f32[3,64,512]{2,1,0:T(8,128)} %get-tuple-element.14), channel_id=1, source_target_pairs={{0,4},{4,8},{8,12},{12,16},{16,20},{20,24},{24,28},{1,5},{5,9},{9,... | collective-permute-start | bytes 1179656 | tf_op jit(solution)/shard_map/ppermute | solution.py:23
  21.2 59.1 %collective-permute-start.1 = (f32[3,64,512]{2,1,0:T(8,128)}, f32[3,64,512]{2,1,0:T(8,128)}, u32[]{:S(2)}, u32[]{:S(2)}) collective-permute-start(f32[3,64,512]{2,1,0:T(8,128)} %get-tuple-element.13), channel_id=1, source_target_pairs={{4,0},{8,4},{12,8},{16,12},{20,16},{24,20},{28,24},{5,1},{9,5},{13... | collective-permute-start | bytes 1179656 | tf_op jit(solution)/shard_map/ppermute | solution.py:24
  22.7 0.5 copy-start.23
  23.9 49.1 %all-to-all-start = ((s32[8,1,12]{2,1,0:T(1,128)}), s32[8,1,12]{2,1,0:T(1,128)S(1)}, u32[]{:S(2)}, u32[]{:S(2)}) async-start(s32[8,1,12]{2,1,0:T(1,128)} %bitcast.6), calls=%async_computation | async-start | bytes 8192 | tf_op jit(solution)/shard_map/all_to_all | solution.py:86
  30.3 120.6 %reduce-scatter.4.cloned.1.call-start = ((), (), s32[]{:S(2)}) async-start(), calls=%async_computation.3 | async-start | bytes 122880
  73.2 0.7 copy-start.9
  73.3 6.8 %copy-start.4 = (f32[16,64,512]{2,1,0:T(8,128)S(1)}, f32[16,64,512]{2,1,0:T(8,128)}, u32[]{:S(2)}) copy-start(f32[16,64,512]{2,1,0:T(8,128)} %param.12) | copy-start | bytes 6291460
  73.5 6.8 %copy-start.11 = (f32[3,64,512]{2,1,0:T(8,128)}, f32[3,64,512]{2,1,0:T(8,128)S(1)}, u32[]{:S(2)}) copy-start(f32[3,64,512]{2,1,0:T(8,128)S(1)} %collective-permute-done.5) | copy-start | bytes 1179652
  74.0 13.4 %collective-permute-start.6 = (f32[22,3,512]{2,1,0:T(4,128)S(1)}, f32[22,3,512]{2,1,0:T(4,128)S(1)}, u32[]{:S(2)}, u32[]{:S(2)}) collective-permute-start(f32[22,3,512]{2,1,0:T(4,128)S(1)} %get-tuple-element.11), channel_id=1, source_target_pairs={{0,1},{1,2},{2,3},{4,5},{5,6},{6,7},{8,9},{9,10},{10,11},{12,13},{... | collective-permute-start | bytes 405512 | tf_op jit(solution)/shard_map/ppermute | solution.py:23
  77.7 9.7 %collective-permute-start.7 = (f32[22,3,512]{2,1,0:T(4,128)S(1)}, f32[22,3,512]{2,1,0:T(4,128)S(1)}, u32[]{:S(2)}, u32[]{:S(2)}) collective-permute-start(f32[22,3,512]{2,1,0:T(4,128)S(1)} %get-tuple-element.12), channel_id=1, source_target_pairs={{1,0},{2,1},{3,2},{5,4},{6,5},{7,6},{9,8},{10,9},{11,10},{13,12},{... | collective-permute-start | bytes 405512 | tf_op jit(solution)/shard_map/ppermute | solution.py:24
  81.4 7.8 %collective-permute-start.2 = (f32[22,3,512]{2,1,0:T(4,128)S(1)}, f32[22,3,512]{2,1,0:T(4,128)S(1)}, u32[]{:S(2)}, u32[]{:S(2)}) collective-permute-start(f32[22,3,512]{2,1,0:T(4,128)S(1)} %get-tuple-element.9), channel_id=1, source_target_pairs={{0,1},{1,2},{2,3},{4,5},{5,6},{6,7},{8,9},{9,10},{10,11},{12,13},{... | collective-permute-start | bytes 405512 | tf_op jit(solution)/shard_map/ppermute | solution.py:23
  85.9 7.5 %collective-permute-start.3 = (f32[22,3,512]{2,1,0:T(4,128)S(1)}, f32[22,3,512]{2,1,0:T(4,128)S(1)}, u32[]{:S(2)}, u32[]{:S(2)}) collective-permute-start(f32[22,3,512]{2,1,0:T(4,128)S(1)} %get-tuple-element.10), channel_id=1, source_target_pairs={{1,0},{2,1},{3,2},{5,4},{6,5},{7,6},{9,8},{10,9},{11,10},{13,12},{... | collective-permute-start | bytes 405512 | tf_op jit(solution)/shard_map/ppermute | solution.py:24
  87.4 0.8 copy-start.5
  87.5 0.9 copy-start.7
  115.7 16.9 %copy-start.2 = (f32[16,64,512]{2,1,0:T(8,128)S(1)}, f32[16,64,512]{2,1,0:T(8,128)}, u32[]{:S(2)}) copy-start(f32[16,64,512]{2,1,0:T(8,128)} %param.13) | copy-start | bytes 6291460
  115.7 16.9 %copy-start.6 = (f32[22,3,512]{2,1,0:T(4,128)S(1)}, f32[22,3,512]{2,1,0:T(4,128)}, u32[]{:S(2)}) copy-start(f32[22,3,512]{2,1,0:T(4,128)} %copy-done.5) | copy-start | bytes 405508
  115.7 16.9 %copy-start.8 = (f32[22,3,512]{2,1,0:T(4,128)S(1)}, f32[22,3,512]{2,1,0:T(4,128)}, u32[]{:S(2)}) copy-start(f32[22,3,512]{2,1,0:T(4,128)} %copy-done.7) | copy-start | bytes 405508
  115.7 16.9 %copy-start.10 = (f32[3,64,512]{2,1,0:T(8,128)S(1)}, f32[3,64,512]{2,1,0:T(8,128)}, u32[]{:S(2)}) copy-start(f32[3,64,512]{2,1,0:T(8,128)} %copy-done.9) | copy-start | bytes 1179652
  115.7 16.9 %copy-start.12 = (f32[3,64,512]{2,1,0:T(8,128)S(1)}, f32[3,64,512]{2,1,0:T(8,128)}, u32[]{:S(2)}) copy-start(f32[3,64,512]{2,1,0:T(8,128)} %copy-done.11) | copy-start | bytes 1179652
  143.5 1.3 copy-start.3
  145.4 11.4 %copy-start.24 = (s32[48]{0:T(128)S(1)}, s32[48]{0:T(128)}, u32[]{:S(2)}) copy-start(s32[48]{0:T(128)} %copy-done.23) | copy-start | bytes 580
  145.4 11.6 %copy-start.13 = (f32[48]{0:T(128)S(1)}, f32[48]{0:T(128)}, u32[]{:S(2)}) copy-start(f32[48]{0:T(128)} %param.19) | copy-start | bytes 580
  145.4 11.6 %copy-start.14 = (f32[48]{0:T(128)S(1)}, f32[48]{0:T(128)}, u32[]{:S(2)}) copy-start(f32[48]{0:T(128)} %param.20) | copy-start | bytes 580
  145.4 11.6 %copy-start.15 = (f32[48]{0:T(128)S(1)}, f32[48]{0:T(128)}, u32[]{:S(2)}) copy-start(f32[48]{0:T(128)} %param.21) | copy-start | bytes 580
  145.4 11.6 %copy-start.16 = (f32[48]{0:T(128)S(1)}, f32[48]{0:T(128)}, u32[]{:S(2)}) copy-start(f32[48]{0:T(128)} %param.17) | copy-start | bytes 580
  145.4 11.6 %copy-start.18 = (f32[48]{0:T(128)S(1)}, f32[48]{0:T(128)}, u32[]{:S(2)}) copy-start(f32[48]{0:T(128)} %param.15) | copy-start | bytes 580
  145.4 11.6 %copy-start.19 = (f32[48]{0:T(128)S(1)}, f32[48]{0:T(128)}, u32[]{:S(2)}) copy-start(f32[48]{0:T(128)} %param.18) | copy-start | bytes 580
  145.4 11.6 %copy-start.20 = (f32[48]{0:T(128)S(1)}, f32[48]{0:T(128)}, u32[]{:S(2)}) copy-start(f32[48]{0:T(128)} %param.16) | copy-start | bytes 580
  147.3 8.3 %all-to-all-start.1 = ((f32[8,1,12]{2,1,0:T(1,128)}), f32[8,1,12]{2,1,0:T(1,128)S(1)}, u32[]{:S(2)}, u32[]{:S(2)}) async-start(f32[8,1,12]{2,1,0:T(1,128)} %bitcast.11), calls=%async_computation.1 | async-start | bytes 8192 | tf_op jit(solution)/shard_map/all_to_all | solution.py:88
Sparse Core Ops, SparseCore 0:
  73.2 19.7 reduce-scatter.3
where the time goes:
time: 165 us; the launch traced here: 164 us
  other arithmetic  52.8 us (32%)
  blocking collectives  40.8 us (25%)
  starting transfers between devices  31.8 us (19%)
  local copies, waits for them, and re-layouts  14.9 us (9%)
  between operations  14.6 us (9%)
  waiting for transfers between devices  8.74 us (5%)
    add x3, other arithmetic, explicit_step(): return centre_p + conductance * flux  47.9 us
    unnamed x1, blocking collectives  40.8 us
    ppermute x4, starting transfers between devices, padded(): before = lax.ppermute(last, axis, up)  16.5 us
    all_to_all x1, starting transfers between devices, fault_pressure_of(): lax.all_to_all(requests, 'gx', split_axis=0, concat_axis=0, tiled=True)  6.32 us
    unnamed x60, local copies, waits for them, and re-layouts  5.8 us
    ppermute x4, starting transfers between devices, padded(): after = lax.ppermute(leading, axis, down)  5.34 us
    slice x2, local copies, waits for them, and re-layouts, padded(): leading = lax.slice_in_dim(value, 0, width, axis=dim)  4.35 us
    ppermute x4, waiting for transfers between devices, padded(): after = lax.ppermute(leading, axis, down)  4.24 us
  transfers between devices with their start and end apart: 11, of which 3 were waited for; matrix products, arithmetic and copies ran while one was open for 37% of the time, Pallas kernels for 0%

commit v1 on v0

v1 whole, which is shorter than its diff:
```python
import functools

import jax
import jax.numpy as jnp
from jax import lax
from jax.experimental import pallas as pl
from jax.experimental.pallas import tpu as pltpu
from jax.sharding import PartitionSpec as P

SWEEPS = 3
LANES = 128
MESH = pl.DeviceIdType.MESH

conductance = 0.15
step_time = 1.0
heal_time = 0.5
friction_ref = 0.6


def step_kernel(
    dims,
    p_hbm,
    k_hbm,
    g_hbm,
    slip_ref,
    aging_ref,
    normal_ref,
    shear_ref,
    direct_ref,
    evolution_ref,
    distance_ref,
    owner_ref,
    cell_ref,
    out_hbm,
    state_ref,
    log_ref,
    p_in,
    k_in,
    g_in,
    out_v,
    root,
    u_a,
    u_b,
    coef_a,
    coef_c,
    inv,
    first_x,
    later_x,
    first_y_send,
    first_y,
    later_y_send,
    later_y,
    slip_send,
    slip_recv,
    req_send,
    req_recv,
    req_smem,
    part_send,
    part_recv,
    ans_send,
    ans_recv,
    load_sem,
    fx_send,
    fx_recv,
    lx_send,
    lx_recv,
    y_send,
    y_recv,
    slip_ssem,
    slip_rsem,
    req_ssem,
    req_rsem,
    part_ssem,
    part_rsem,
    ans_ssem,
    ans_rsem,
):
    n_gx, n_gy, cx, cy, nz, tri, rows, cols, cap, cap_pad = dims
    nb = nz // LANES
    yp = cy + 8
    gx, gy = lax.axis_index("gx"), lax.axis_index("gy")
    dev = gx * n_gy + gy
    slip_gy = dev // n_gx
    slip_slot = dev % n_gx
    lane = lax.broadcasted_iota(jnp.int32, (1, LANES), 1)

    load_k = pltpu.make_async_copy(k_hbm, k_in, load_sem.at[0])
    load_p = pltpu.make_async_copy(p_hbm, p_in, load_sem.at[1])
    load_g = pltpu.make_async_copy(g_hbm, g_in, load_sem.at[2])
    load_k.start()
    load_p.start()
    load_g.start()

    barrier = pltpu.get_barrier_semaphore()

    def greet(x, y):
        pl.semaphore_signal(barrier, inc=1, device_id={"gx": x, "gy": y}, device_id_type=MESH)

    for off in range(1, n_gx):
        greet((gx + off) % n_gx, gy)
    for off in range(1, n_gy):
        greet(gx, (gy + off) % n_gy)
    for i in range(n_gx):
        source = gy * n_gx + i

        @pl.when(source != dev)
        def _():
            greet(source // n_gy, source % n_gy)

    zero = jnp.zeros((8, LANES), jnp.float32)
    n_col = (cx + 2) * nb
    for ref in (root, u_a, u_b):

        def clear_pad(c, _, ref=ref):
            ref[pl.ds(pl.multiple_of(c * yp, 8), 8), :] = zero
            return 0

        lax.fori_loop(0, n_col + 1, clear_pad, 0)

        def clear_end(c, _, ref=ref):
            ref[pl.ds(pl.multiple_of(c * 8, 8), 8), :] = zero
            ref[pl.ds(pl.multiple_of((cx + 1) * nb * yp + c * 8, 8), 8), :] = zero
            return 0

        lax.fori_loop(0, nb * yp // 8, clear_end, 0)

    slip_send[...] = jnp.zeros_like(slip_send)
    slip_send[0, :, :tri] = slip_ref[...]

    owner_row = owner_ref[...]
    cell_row = cell_ref[...]
    t_row = lax.broadcasted_iota(jnp.int32, (tri, tri), 1)
    t_col = lax.broadcasted_iota(jnp.int32, (tri, tri), 0)
    eye = t_row == t_col
    owner_wide = jnp.broadcast_to(owner_row, (tri, tri))
    owner_col = jnp.sum(jnp.where(eye, owner_wide, 0), axis=1, keepdims=True)
    cell_col = jnp.sum(
        jnp.where(eye, jnp.broadcast_to(cell_row, (tri, tri)), 0), axis=1, keepdims=True
    )
    same = owner_col == owner_wide
    one_below = jnp.where(same & (t_row < t_col), 1, 0)
    one_above = jnp.where(same & (t_col < t_row), 1, 0)
    rank_col = jnp.sum(one_below, axis=1, keepdims=True)
    rank_row = jnp.sum(one_above, axis=0, keepdims=True)
    slot_col = owner_col * cap + rank_col
    slot_row = owner_row * cap_pad + rank_row
    width = req_send.shape[-1]
    slot_lane = lax.broadcasted_iota(jnp.int32, (tri, width), 1)
    req_send[0] = jnp.sum(jnp.where(slot_col == slot_lane, cell_col, 0), axis=0, keepdims=True)
    req_recv[pl.ds(gx, 1)] = req_send[...]

    @pl.when(slip_gy == gy)
    def _():
        slip_recv[pl.ds(slip_slot, 1)] = slip_send[...]

    alone = jnp.where(slip_gy == gy, 1, 0)
    pl.semaphore_wait(barrier, n_gx - 1 + n_gy - 1 + n_gx - alone)

    def remote(src, dst, send, recv, x, y):
        return pltpu.make_async_remote_copy(
            src_ref=src,
            dst_ref=dst,
            send_sem=send,
            recv_sem=recv,
            device_id={"gx": x, "gy": y},
            device_id_type=MESH,
        )

    has_lo_x, has_hi_x = gx > 0, gx < n_gx - 1
    has_lo_y, has_hi_y = gy > 0, gy < n_gy - 1
    lo_x, hi_x = jnp.maximum(gx - 1, 0), jnp.minimum(gx + 1, n_gx - 1)
    lo_y, hi_y = jnp.maximum(gy - 1, 0), jnp.minimum(gy + 1, n_gy - 1)

    def first_x_copy(side, which):
        src = (k_hbm, p_hbm)[which].at[cx - 1 if side == 0 else 0]
        return remote(
            src,
            first_x.at[side, which],
            fx_send.at[side, which],
            fx_recv.at[side, which],
            hi_x if side == 0 else lo_x,
            gy,
        )

    def later_x_copy(side, turn, ref):
        plane = cx if side == 0 else 1
        src = ref.at[pl.ds(plane * nb * yp + 8, nb * yp - 8), :]
        return remote(
            src,
            later_x.at[turn, side],
            lx_send.at[turn, side],
            lx_recv.at[turn, side],
            hi_x if side == 0 else lo_x,
            gy,
        )

    def y_copy(side, turn):
        if turn == 0:
            src, dst = first_y_send.at[side], first_y.at[side]
        else:
            src, dst = later_y_send.at[turn - 1, side], later_y.at[turn - 1, side]
        return remote(
            src,
            dst,
            y_send.at[turn, side],
            y_recv.at[turn, side],
            gx,
            hi_y if side == 0 else lo_y,
        )

    send_when_x = (has_hi_x, has_lo_x)
    recv_when_x = (has_lo_x, has_hi_x)
    send_when_y = (has_hi_y, has_lo_y)
    recv_when_y = (has_lo_y, has_hi_y)

    for side in range(2):

        @pl.when(send_when_x[side])
        def _():
            first_x_copy(side, 0).start()
            first_x_copy(side, 1).start()

    def req_copy(off):
        return remote(
            req_send.at[0],
            req_recv.at[gx],
            req_ssem.at[off],
            req_rsem.at[off],
            (gx + off) % n_gx,
            gy,
        )

    def slip_copy(g):
        return remote(
            slip_send.at[0],
            slip_recv.at[slip_slot],
            slip_ssem.at[g],
            slip_rsem.at[slip_slot],
            g,
            slip_gy,
        )

    for g in range(n_gx):

        @pl.when((g != gx) | (slip_gy != gy))
        def _():
            slip_copy(g).start()

    for off in range(1, n_gx):
        req_copy(off).start()

    load_k.wait()
    load_p.wait()

    def prepare(x, _):
        for j in range(nb):
            k = k_in[x, :, j * LANES : (j + 1) * LANES]
            p = p_in[x, :, j * LANES : (j + 1) * LANES]
            r = lax.rsqrt(k)
            s = k * r
            at = pl.ds(pl.multiple_of(((x + 1) * nb + j) * yp + 8, 8), cy)
            dense = pl.ds(pl.multiple_of((x * nb + j) * cy, 8), cy)
            root[at, :] = s
            u_a[at, :] = s * p
            inv[dense, :] = r
            coef_c[dense, :] = conductance * k
        return 0

    lax.fori_loop(0, cx, prepare, 0)

    n_face = cx * nb

    def face(y):
        return pl.ds(nb * yp + 8 + y, n_face, stride=yp)

    def dense_face(y):
        return pl.ds(y, n_face, stride=cy)

    y_of = (cy - 1, 0)
    for side in range(2):
        first_y_send[side, 0] = root[face(y_of[side]), :]
        first_y_send[side, 1] = u_a[face(y_of[side]), :]
    for side in range(2):

        @pl.when(send_when_y[side])
        def _():
            y_copy(side, 0).start()

    chunk = 16

    def around(ref, x, y0):
        here, sums = [], []
        for j in range(nb):
            at = ((x + 1) * nb + j) * yp + 8 + y0
            here.append(ref[pl.ds(pl.multiple_of(at, 8), chunk), :])
        for j in range(nb):
            at = ((x + 1) * nb + j) * yp + 8 + y0
            before = here[j - 1] if j > 0 else 0.0
            after = here[j + 1] if j < nb - 1 else 0.0
            left = pltpu.roll(jnp.where(lane == LANES - 1, before, here[j]), 1, 1)
            right = pltpu.roll(jnp.where(lane == 0, after, here[j]), LANES - 1, 1)
            total = ref[pl.ds(pl.multiple_of(at + nb * yp, 8), chunk), :]
            total = total + ref[pl.ds(pl.multiple_of(at - nb * yp, 8), chunk), :]
            total = total + (ref[pl.ds(at + 1, chunk), :] + ref[pl.ds(at - 1, chunk), :])
            sums.append(total + (left + right))
        return here, sums

    def sweep(turn, src, dst):
        def plane(x, _):
            for y0 in range(0, cy, chunk):
                here, sums = around(src, x, y0)
                if turn == 0:
                    roots, root_sums = around(root, x, y0)
                for j in range(nb):
                    dense = pl.ds(pl.multiple_of((x * nb + j) * cy + y0, 8), chunk)
                    if turn == 0:
                        a = 1.0 - conductance * (roots[j] * root_sums[j])
                        coef_a[dense, :] = a
                    else:
                        a = coef_a[dense, :]
                    new = a * here[j] + coef_c[dense, :] * sums[j]
                    if turn < SWEEPS - 1:
                        at = ((x + 1) * nb + j) * yp + 8 + y0
                        dst[pl.ds(pl.multiple_of(at, 8), chunk), :] = new
                    else:
                        out_v[x, y0 : y0 + chunk, j * LANES : (j + 1) * LANES] = (
                            new * inv[dense, :]
                        )
            return 0

        lax.fori_loop(0, cx, plane, 0)

    def fix_x(turn, side, src, dst):
        x = 0 if side == 0 else cx - 1
        for j in range(nb):
            at = pl.ds(((x + 1) * nb + j) * yp + 8, cy)
            dense = pl.ds((x * nb + j) * cy, cy)
            if turn == 0:
                k = first_x[side, 0, :, j * LANES : (j + 1) * LANES]
                s = k * lax.rsqrt(k)
                halo = s * first_x[side, 1, :, j * LANES : (j + 1) * LANES]
                less = conductance * (root[at, :] * s)
                coef_a[dense, :] = coef_a[dense, :] - less
                dst[at, :] = dst[at, :] + (coef_c[dense, :] * halo - less * src[at, :])
            else:
                halo = later_x[turn - 1, side, pl.ds(j * yp, cy), :]
                if turn < SWEEPS - 1:
                    dst[at, :] = dst[at, :] + coef_c[dense, :] * halo
                else:
                    cols_j = slice(j * LANES, (j + 1) * LANES)
                    out_v[x, :, cols_j] = out_v[x, :, cols_j] + coef_c[dense, :] * inv[
                        dense, :
                    ] * halo

    def fix_y(turn, side, src, dst):
        y = 0 if side == 0 else cy - 1
        at, dense = face(y), dense_face(y)
        if turn == 0:
            s, halo = first_y[side, 0], first_y[side, 1]
            less = conductance * (root[at, :] * s)
            coef_a[dense, :] = coef_a[dense, :] - less
            dst[at, :] = dst[at, :] + (coef_c[dense, :] * halo - less * src[at, :])
        else:
            halo = later_y[turn - 1, side]
            if turn < SWEEPS - 1:
                dst[at, :] = dst[at, :] + coef_c[dense, :] * halo
            else:
                later_y[turn - 1, side] = coef_c[dense, :] * inv[dense, :] * halo
                for x in range(cx):
                    for j in range(nb):
                        cols_j = slice(j * LANES, (j + 1) * LANES)
                        row = x * nb + j
                        out_v[x, y : y + 1, cols_j] = (
                            out_v[x, y : y + 1, cols_j] + later_y[turn - 1, side, row : row + 1, :]
                        )

    def take_halos(turn, src, dst):
        for side in range(2):

            @pl.when(recv_when_y[side])
            def _():
                y_copy(side, turn).wait_recv()
                fix_y(turn, side, src, dst)

        for side in range(2):

            @pl.when(recv_when_x[side])
            def _():
                if turn == 0:
                    first_x_copy(side, 0).wait_recv()
                    first_x_copy(side, 1).wait_recv()
                else:
                    later_x_copy(side, turn - 1, src).wait_recv()
                fix_x(turn, side, src, dst)

    def send_halos(turn, ref):
        for side in range(2):
            later_y_send[turn - 1, side] = ref[face(y_of[side]), :]
        for side in range(2):

            @pl.when(send_when_x[side])
            def _():
                later_x_copy(side, turn - 1, ref).start()

        for side in range(2):

            @pl.when(send_when_y[side])
            def _():
                y_copy(side, turn).start()

    sweep(0, u_a, u_b)
    take_halos(0, u_a, u_b)
    send_halos(1, u_b)

    for i in range(n_gx):

        @pl.when(gy * n_gx + i != dev)
        def _():
            remote(
                slip_send.at[0], slip_recv.at[i], slip_ssem.at[0], slip_rsem.at[i], gx, gy
            ).wait_recv()

    n_cb = cols // LANES
    segment = [jnp.zeros((1, LANES), jnp.float32) for _ in range(n_cb)]
    for i in range(n_gx):
        first, shift = (i * tri) // LANES, (i * tri) % LANES
        row = slip_recv[i]
        if shift:
            row = pltpu.roll(row, shift, 1)
        segment[first] = segment[first] + jnp.where(lane >= shift, row, 0.0)
        if shift + tri > LANES:
            segment[first + 1] = segment[first + 1] + jnp.where(lane < shift, row, 0.0)
    eye_f = lax.broadcasted_iota(jnp.int32, (tri, LANES), 0) == lax.broadcasted_iota(
        jnp.int32, (tri, LANES), 1
    )
    for part in range(n_gy):
        for comp in range(2):
            total = jnp.zeros((tri, LANES), jnp.float32)
            for b in range(n_cb):
                block = g_tile(g_in, load_g, part, comp, b, tri)
                total = total + block * segment[b]
            sums = jnp.sum(total, axis=1, keepdims=True)
            part_send[part, comp : comp + 1, :] = jnp.sum(
                jnp.where(eye_f, sums, 0.0), axis=0, keepdims=True
            )

    def part_copy(off):
        to = (gy + off) % n_gy
        return remote(
            part_send.at[to], part_recv.at[gy], part_ssem.at[off], part_rsem.at[off], gx, to
        )

    part_recv[pl.ds(gy, 1)] = part_send[pl.ds(gy, 1)]
    for off in range(1, n_gy):
        part_copy(off).start()

    sweep(1, u_b, u_a)
    take_halos(1, u_b, u_a)
    send_halos(2, u_a)
    for off in range(1, n_gx):
        remote(
            req_send.at[0],
            req_recv.at[(gx + n_gx - off) % n_gx],
            req_ssem.at[off],
            req_rsem.at[off],
            gx,
            gy,
        ).wait_recv()
    to_smem = pltpu.make_async_copy(req_recv, req_smem, load_sem.at[3])
    to_smem.start()
    ans_send[...] = jnp.zeros_like(ans_send)
    sweep(2, u_a, None)

    for off in range(1, n_gy):
        remote(
            part_send.at[0],
            part_recv.at[(gy + n_gy - off) % n_gy],
            part_ssem.at[off],
            part_rsem.at[off],
            gx,
            gy,
        ).wait_recv()
    rates = part_recv[0]
    for other in range(1, n_gy):
        rates = rates + part_recv[other]
    shear = shear_ref[...] + step_time * rates[0:1, :tri]
    loaded = normal_ref[...] + step_time * rates[1:2, :tri]
    distance = distance_ref[...]
    ratio = distance / slip_ref[...]
    state_next = ratio + (aging_ref[...] - ratio) * jnp.exp(-heal_time / ratio)
    state_ref[...] = state_next
    evolved = evolution_ref[...] * jnp.log(state_next / distance)
    to_smem.wait()

    take_halos(2, u_a, None)
    store = pltpu.make_async_copy(out_v, out_hbm, load_sem.at[4])
    store.start()

    lane_z = lax.broadcasted_iota(jnp.int32, (1, nz), 1)

    def answer(source, _):
        for s in range(cap):
            c = req_smem[source, 0, gx * cap + s]
            row = out_v[c // (cy * nz), pl.ds((c // nz) % cy, 1), :]
            row = jnp.where(lane_z == c % nz, row, 0.0)
            picked = row[:, :LANES]
            for j in range(1, nb):
                picked = picked + row[:, j * LANES : (j + 1) * LANES]
            ans_send[source, s : s + 1, :] = picked
        return 0

    lax.fori_loop(0, n_gx, answer, 0)

    def ans_copy(off):
        to = (gx + off) % n_gx
        return remote(
            ans_send.at[to], ans_recv.at[gx], ans_ssem.at[off], ans_rsem.at[off], to, gy
        )

    for off in range(1, n_gx):
        ans_copy(off).start()
    ans_recv[pl.ds(gx, 1)] = ans_send[pl.ds(gx, 1)]
    for off in range(1, n_gx):
        remote(
            ans_send.at[0],
            ans_recv.at[(gx + n_gx - off) % n_gx],
            ans_ssem.at[off],
            ans_rsem.at[off],
            gx,
            gy,
        ).wait_recv()
    n_slot = n_gx * cap_pad
    answers = jnp.sum(ans_recv[...].reshape(n_slot, LANES), axis=1, keepdims=True)
    mine = lax.broadcasted_iota(jnp.int32, (n_slot, tri), 0) == slot_row
    fault = jnp.sum(jnp.where(mine, answers, 0.0), axis=0, keepdims=True)
    log_ref[...] = (shear / (loaded - fault) - friction_ref - evolved) / direct_ref[...]

    for side in range(2):

        @pl.when(send_when_x[side])
        def _():
            first_x_copy(side, 0).wait_send()
            first_x_copy(side, 1).wait_send()
            later_x_copy(side, 0, u_b).wait_send()
            later_x_copy(side, 1, u_a).wait_send()

        @pl.when(send_when_y[side])
        def _():
            for turn in range(SWEEPS):
                y_copy(side, turn).wait_send()

    for g in range(n_gx):

        @pl.when((g != gx) | (slip_gy != gy))
        def _():
            slip_copy(g).wait_send()

    for off in range(1, n_gx):
        req_copy(off).wait_send()
        ans_copy(off).wait_send()
    for off in range(1, n_gy):
        part_copy(off).wait_send()
    store.wait()


def g_tile(g_in, load_g, part, comp, b, tri):
    if part == 0 and comp == 0 and b == 0:
        load_g.wait()
    return g_in[comp, part * tri : (part + 1) * tri, b * LANES : (b + 1) * LANES]


def local(
    pressure,
    permeability,
    kernel,
    slip_rate,
    aging_state,
    normal_stress,
    shear_stress,
    direct_effect,
    evolution_effect,
    slip_distance,
    tri_owner,
    tri_cell,
):
    n_gx, n_gy = lax.axis_size("gx"), lax.axis_size("gy")
    cx, cy, nz = pressure.shape
    tri = slip_rate.shape[0]
    _, rows, cols = kernel.shape
    cap = max(2, 2 * tri // n_gx)
    cap_pad = -(-cap // 8) * 8
    nb = nz // LANES
    yp = cy + 8
    padded = ((cx + 2) * nb * yp + 8, LANES)
    dense = (cx * nb * cy, LANES)
    width = -(-n_gx * cap // LANES) * LANES
    dims = (n_gx, n_gy, cx, cy, nz, tri, rows, cols, cap, cap_pad)
    f32, i32 = jnp.float32, jnp.int32
    dma = pltpu.SemaphoreType.DMA
    vec = lambda a: a.reshape(1, tri)
    any_spec = pl.BlockSpec(memory_space=pl.ANY)
    vmem_spec = pl.BlockSpec(memory_space=pltpu.VMEM)
    out, state, log = pl.pallas_call(
        functools.partial(step_kernel, dims),
        out_shape=(
            jax.ShapeDtypeStruct(pressure.shape, f32),
            jax.ShapeDtypeStruct((1, tri), f32),
            jax.ShapeDtypeStruct((1, tri), f32),
        ),
        in_specs=[any_spec] * 3 + [vmem_spec] * 9,
        out_specs=(any_spec, vmem_spec, vmem_spec),
        scratch_shapes=[
            pltpu.VMEM(pressure.shape, f32),
            pltpu.VMEM(pressure.shape, f32),
            pltpu.VMEM(kernel.shape, f32),
            pltpu.VMEM(pressure.shape, f32),
            pltpu.VMEM(padded, f32),
            pltpu.VMEM(padded, f32),
            pltpu.VMEM(padded, f32),
            pltpu.VMEM(dense, f32),
            pltpu.VMEM(dense, f32),
            pltpu.VMEM(dense, f32),
            pltpu.VMEM((2, 2, cy, nz), f32),
            pltpu.VMEM((SWEEPS - 1, 2, nb * yp - 8, LANES), f32),
            pltpu.VMEM((2, 2, cx * nb, LANES), f32),
            pltpu.VMEM((2, 2, cx * nb, LANES), f32),
            pltpu.VMEM((SWEEPS - 1, 2, cx * nb, LANES), f32),
            pltpu.VMEM((SWEEPS - 1, 2, cx * nb, LANES), f32),
            pltpu.VMEM((1, 1, LANES), f32),
            pltpu.VMEM((n_gx, 1, LANES), f32),
            pltpu.VMEM((1, 1, width), i32),
            pltpu.VMEM((n_gx, 1, width), i32),
            pltpu.SMEM((n_gx, 1, width), i32),
            pltpu.VMEM((n_gy, 2, LANES), f32),
            pltpu.VMEM((n_gy, 2, LANES), f32),
            pltpu.VMEM((n_gx, cap_pad, LANES), f32),
            pltpu.VMEM((n_gx, cap_pad, LANES), f32),
            dma((5,)),
            dma((2, 2)),
            dma((2, 2)),
            dma((SWEEPS - 1, 2)),
            dma((SWEEPS - 1, 2)),
            dma((SWEEPS, 2)),
            dma((SWEEPS, 2)),
            dma((n_gx,)),
            dma((n_gx,)),
            dma((n_gx,)),
            dma((n_gx,)),
            dma((n_gy,)),
            dma((n_gy,)),
            dma((n_gx,)),
            dma((n_gx,)),
        ],
        compiler_params=pltpu.CompilerParams(collective_id=0, has_side_effects=True),
        name="fault_step",
    )(
        pressure,
        permeability,
        kernel,
        vec(slip_rate),
        vec(aging_state),
        vec(normal_stress),
        vec(shear_stress),
        vec(direct_effect),
        vec(evolution_effect),
        vec(slip_distance),
        vec(tri_owner),
        vec(tri_cell),
    )
    return out, state.reshape(tri), log.reshape(tri)


def solution(mesh):
    fault = P(("gx", "gy"))
    field = P("gx", "gy", None)
    in_specs = (field, field, P(None, "gx", "gy")) + (fault,) * 7 + (P(("gx", "gy"), None), fault)
    out_specs = (field, fault, fault)
    return jax.shard_map(local, mesh=mesh, in_specs=in_specs, out_specs=out_specs, check_vma=False)
```

time: 165 us -> 33.8 us (0.20)
  other arithmetic: 52.8 us -> 0 us
  blocking collectives: 40.8 us -> 0 us
  starting transfers between devices: 31.8 us -> 0 us
  Pallas kernels: 0 us -> 28.8 us
  between operations: 14.6 us -> 0.66 us
  local copies, waits for them, and re-layouts: 14.9 us -> 4.18 us
  waiting for transfers between devices: 8.74 us -> 0 us
    add x3 -> x0, other arithmetic: 47.9 us -> none  [explicit_step(): return centre_p + conductance * flux]
    unnamed x1 -> x0, blocking collectives: 40.8 us -> none
    pallas_call x0 -> x1, Pallas kernels: none -> 28.8 us  [local(): pl.pallas_call(functools.partial(step_kernel, dims), out_shape=(jax.Shape...]
    ppermute x8 -> x0, starting transfers between devices: 21.9 us -> none  [the longest x4 16.5 us: padded(): before = lax.ppermute(last, axis, up)]
    all_to_all x2 -> x0, starting transfers between devices: 9.89 us -> none  [the longest x1 6.32 us: fault_pressure_of(): lax.all_to_all(requests, 'gx', split_axis=0, concat_axis=0, tiled=True)]
    slice x5 -> x0, local copies, waits for them, and re-layouts: 5.38 us -> none  [the longest x2 4.35 us: padded(): leading = lax.slice_in_dim(value, 0, width, axis=dim)]
    ppermute x8 -> x0, waiting for transfers between devices: 5.08 us -> none  [the longest x4 4.24 us: padded(): after = lax.ppermute(leading, axis, down)]
    all_to_all x2 -> x0, waiting for transfers between devices: 3.63 us -> none  [the longest x1 3.63 us: fault_pressure_of(): lax.all_to_all(values, 'gx', split_axis=0, concat_axis=0, tiled=True)]
  transfers between devices with their start and end apart: 11 -> 0, of which waited for: 3 -> 0; matrix products, arithmetic and copies ran while one was open for 37% -> 0% of each run, Pallas kernels for 0% -> 0%
where the time goes in v1:
time: 33.8 us; the launch traced here: 33.7 us
  Pallas kernels  28.8 us (85%)
  local copies, waits for them, and re-layouts  4.18 us (12%)
  between operations  0.66 us (2%)
    pallas_call x1, Pallas kernels, local(): pl.pallas_call(functools.partial(step_kernel, dims), out_shape=(jax.Shape...  28.8 us
    unnamed x7, local copies, waits for them, and re-layouts  4.18 us

profile of v1, /device:TPU:0, one launch (start us, length us, event | category | flops | bytes accessed | tf_op | source)
XLA Modules:
  0.0 33.7 jit_solution(3464530929856837727)
XLA Ops:
  0.6 28.8 %fault_step.1 = (f32[16,64,512]{2,1,0:T(8,128)}, f32[1,48]{1,0:T(1,128)}, f32[1,48]{1,0:T(1,128)}) custom-call(f32[16,64,512]{2,1,0:T(8,128)} %p_hbm.1, f32[16,64,512]{2,1,0:T(8,128)} %k_hbm.1, f32[2,192,384]{2,1,0:T(8,128)} %g_hbm.1, f32[1,48]{1,0:T(1,128)} %bitcast.11, f32[1,48]{1,0:T(1,128)} %bitcast.12, f32[1,48]{1,0:T(1,128)} %bitcast.13, ...), custom_call_target="tpu_custom_call" | custom-call | tf_op jit(solution)/shard_map/fault_step/pallas_call | solution.py:603
  29.5 0.0 copy-start.1
  29.5 0.0 copy-start
  29.5 3.1 %copy.18 = f32[16,64,512]{2,1,0:T(8,128)} copy(f32[16,64,512]{2,1,0:T(8,128)} %get-tuple-element.12) | data formatting | bytes 4194304
  32.7 0.0 copy-done.1
  32.7 0.5 %copy.19 = f32[48]{0:T(128)} copy(f32[48]{0:T(128)S(1)} %bitcast.21) | data formatting | bytes 384
  33.2 0.0 copy-done
  33.2 0.5 %copy.20 = f32[48]{0:T(128)} copy(f32[48]{0:T(128)S(1)} %bitcast.20) | data formatting | bytes 384
Async XLA Ops:
  29.5 3.2 %copy-start.1 = (f32[1,48]{1,0:T(1,128)S(1)}, f32[1,48]{1,0:T(1,128)}, u32[]{:S(2)}) copy-start(f32[1,48]{1,0:T(1,128)} %get-tuple-element.7) | copy-start | bytes 580
  29.5 3.7 %copy-start = (f32[1,48]{1,0:T(1,128)S(1)}, f32[1,48]{1,0:T(1,128)}, u32[]{:S(2)}) copy-start(f32[1,48]{1,0:T(1,128)} %get-tuple-element.8) | copy-start | bytes 580

commit v2 on v1

--- a/solution.py
+++ b/solution.py
@@ -501,8 +501,8 @@
     def answer(source, _):
         for s in range(cap):
             c = req_smem[source, 0, gx * cap + s]
-            row = out_v[c // (cy * nz), pl.ds((c // nz) % cy, 1), :]
-            row = jnp.where(lane_z == c % nz, row, 0.0)
+            row = out_v[part_of(c, cy * nz), pl.ds(rest_of(part_of(c, nz), cy), 1), :]
+            row = jnp.where(lane_z == rest_of(c, nz), row, 0.0)
             picked = row[:, :LANES]
             for j in range(1, nb):
                 picked = picked + row[:, j * LANES : (j + 1) * LANES]
@@ -561,6 +561,36 @@
     for off in range(1, n_gy):
         part_copy(off).wait_send()
     store.wait()
+
+
+def part_of(value, size):
+    if size & (size - 1) == 0:
+        return lax.shift_right_logical(value, jnp.int32(size.bit_length() - 1))
+    return lax.div(value, jnp.int32(size))
+
+
+def rest_of(value, size):
+    if size & (size - 1) == 0:
+        return value & (size - 1)
+    return lax.rem(value, jnp.int32(size))
+
+
+def copy_kernel(p_hbm, state_in, log_in, out_hbm, state_ref, log_ref, buf, in_sem, out_sem):
+    planes = p_hbm.shape[0]
+    n = in_sem.shape[0]
+    reads, writes = [], []
+    for i in range(n):
+        part = pl.ds(i * planes // n, planes // n)
+        reads.append(pltpu.make_async_copy(p_hbm.at[part], buf.at[part], in_sem.at[i]))
+        writes.append(pltpu.make_async_copy(buf.at[part], out_hbm.at[part], out_sem.at[i]))
+        reads[-1].start()
+    state_ref[...] = state_in[...]
+    log_ref[...] = log_in[...]
+    for i in range(n):
+        reads[i].wait()
+        writes[i].start()
+    for i in range(n):
+        writes[i].wait()
 
 
 def g_tile(g_in, load_g, part, comp, b, tri):
@@ -667,6 +697,19 @@
         vec(tri_owner),
         vec(tri_cell),
     )
+    pieces = cx if cx < 8 else 8 if cx % 8 == 0 else 1
+    out, state, log = pl.pallas_call(
+        copy_kernel,
+        out_shape=(
+            jax.ShapeDtypeStruct(pressure.shape, f32),
+            jax.ShapeDtypeStruct((1, tri), f32),
+            jax.ShapeDtypeStruct((1, tri), f32),
+        ),
+        in_specs=[any_spec, vmem_spec, vmem_spec],
+        out_specs=(any_spec, vmem_spec, vmem_spec),
+        scratch_shapes=[pltpu.VMEM(pressure.shape, f32), dma((pieces,)), dma((pieces,))],
+        name="write_out",
+    )(out, state, log)
     return out, state.reshape(tri), log.reshape(tri)
 
 

time: 33.8 us -> 32.3 us (0.956)
  local copies, waits for them, and re-layouts: 4.18 us -> 0 us
  Pallas kernels: 28.8 us -> 31.5 us
    unnamed x7 -> x0, local copies, waits for them, and re-layouts: 4.18 us -> none
    pallas_call x0 -> x1, Pallas kernels: none -> 3.52 us  [local(): pl.pallas_call(copy_kernel, out_shape=(jax.ShapeDtypeStruct(pressure.shap...]
    pallas_call x1, Pallas kernels: 28.8 us -> 28 us  [local(): pl.pallas_call(functools.partial(step_kernel, dims), out_shape=(jax.Shape...]
where the time goes in v2:
time: 32.3 us; the launch traced here: 32.1 us
  Pallas kernels  31.5 us (98%)
  between operations  0.64 us (2%)
    pallas_call x1, Pallas kernels, local(): pl.pallas_call(functools.partial(step_kernel, dims), out_shape=(jax.Shape...  28 us
    pallas_call x1, Pallas kernels, local(): pl.pallas_call(copy_kernel, out_shape=(jax.ShapeDtypeStruct(pressure.shap...  3.52 us

profile of v2, /device:TPU:0, one launch (start us, length us, event | category | flops | bytes accessed | tf_op | source)
XLA Modules:
  0.0 32.1 jit_solution(12346649649127771803)
XLA Ops:
  0.6 28.0 %fault_step.1 = (f32[16,64,512]{2,1,0:T(8,128)}, f32[1,48]{1,0:T(1,128)}, f32[1,48]{1,0:T(1,128)}) custom-call(f32[16,64,512]{2,1,0:T(8,128)} %p_hbm.1, f32[16,64,512]{2,1,0:T(8,128)} %k_hbm.1, f32[2,192,384]{2,1,0:T(8,128)} %g_hbm.1, f32[1,48]{1,0:T(1,128)} %bitcast.11, f32[1,48]{1,0:T(1,128)} %bitcast.12, f32[1,48]{1,0:T(1,128)} %bitcast.13, ...), custom_call_target="tpu_custom_call" | custom-call | tf_op jit(solution)/shard_map/fault_step/pallas_call | solution.py:633
  28.6 3.5 %write_out.1 = (f32[16,64,512]{2,1,0:T(8,128)}, f32[1,48]{1,0:T(1,128)}, f32[1,48]{1,0:T(1,128)}) custom-call(f32[16,64,512]{2,1,0:T(8,128)} %get-tuple-element.9.p_hbm, f32[1,48]{1,0:T(1,128)} %get-tuple-element.10.state_in, f32[1,48]{1,0:T(1,128)} %get-tuple-element.11.log_in), custom_call_target="tpu_custom_call" | custom-call | tf_op jit(solution)/shard_map/write_out/pallas_call | solution.py:701
